TPU v7x, 512 devices: a whole 4x4x16 slice. The times are simulated.
512 devices in a mesh: freq: 16 (over y, x_hi, core), gx: 32 (over z, x_lo).
Axes of the slice: x: 4 (x_hi: 2, x_lo: 2; x = x_hi * 2 + x_lo), y: 4, z: 16, core: 2. Of those that a mesh axis runs over, the one named last changes fastest.
Arguments:
- sigma_h: float32 [128, 64, 256], P('gx'), may hold values from 0.3 to 3
- sigma_v: float32 [128, 64, 256], P('gx'), may hold values from 0.3 to 3
- wave_scale: float32 [16], P('freq'), may hold values from 0.25 to 4
- field_start: bfloat16 [16, 2, 3, 128, 64, 256], P('freq', None, None, 'gx'), may hold values from -6 to 6
- adjoint_start: bfloat16 [16, 2, 3, 128, 64, 256], P('freq', None, None, 'gx'), may hold values from -6 to 6
- observed: bfloat16 [16, 2, 3, 128, 64, 256], P('freq', None, None, 'gx'), may hold values from -6 to 6
- tx_count: int32 [1], replicated, may hold values from 1 to 64
- tx_cells: int32 [64], replicated, may hold values from 0 to 2097151
Outputs:
- gradient: float32 [2, 128, 64, 256], P(None, 'gx', 'freq')
- final_field: float32 [16, 2, 3, 128, 64, 256], P('freq', None, None, 'gx')
All inputs are finite; a program needn't handle non-finite values.
Results may differ from a plain program's by a relative error of at most 0.0003.
Values sent between devices are 32-bit elements; how exact they have to be, the bound alone decides.
No kernel may reach another device: no remote copies, remote signals or barrier semaphores. Data moves between devices by JAX's collectives and lax.ppermute only.
A program may use at most 64 MiB of HBM per device.

v0:
```python
import jax
import jax.numpy as jnp
from jax import lax
from jax.sharding import PartitionSpec as P

ITERS = 2
THETA = 0.5
SOURCE_GAIN = 8.0


def padded_2(cells, sides, width):
    for axis, dim in sides:
        count = lax.axis_size(axis)
        ends = count - 1
        head = lax.slice_in_dim(cells, 0, width, axis=dim)
        tail = lax.slice_in_dim(cells, cells.shape[dim] - width, cells.shape[dim], axis=dim)
        cells = jnp.concatenate(
            [
                lax.ppermute(tail, axis, [(i, (i + 1) % count) for i in range(ends)]),
                cells,
                lax.ppermute(head, axis, [((i + 1) % count, i) for i in range(ends)]),
            ],
            axis=dim,
        )
    return cells


def ahead_diff(values, along):
    along = values.ndim + along
    widths = [(0, 0)] * values.ndim
    widths[along] = (0, 1)
    padded = jnp.pad(values, widths)
    return lax.slice_in_dim(padded, 1, values.shape[along] + 1, axis=along) - values


def behind_diff(values, along):
    along = values.ndim + along
    widths = [(0, 0)] * values.ndim
    widths[along] = (1, 0)
    padded = jnp.pad(values, widths)
    return values - lax.slice_in_dim(padded, 0, values.shape[along], axis=along)


def curl_masked(efield, inside):
    comp_x = efield[..., 0, :, :, :]
    comp_y = efield[..., 1, :, :, :]
    comp_z = efield[..., 2, :, :, :]
    twist_x = (ahead_diff(comp_z, -2) - ahead_diff(comp_y, -1)) * inside
    twist_y = (ahead_diff(comp_x, -1) - ahead_diff(comp_z, -3)) * inside
    twist_z = (ahead_diff(comp_y, -3) - ahead_diff(comp_x, -2)) * inside
    back_x = behind_diff(twist_z, -2) - behind_diff(twist_y, -1)
    back_y = behind_diff(twist_x, -1) - behind_diff(twist_z, -3)
    back_z = behind_diff(twist_y, -3) - behind_diff(twist_x, -2)
    return jnp.stack([back_x, back_y, back_z], axis=-4)


def relax(efield, curled, source_term, sig_pair, wave_scale):
    sigma_comp = jnp.stack([sig_pair[0], sig_pair[0], sig_pair[1]])
    coupling = wave_scale[:, None, None, None, None] * sigma_comp[None]
    real_part = efield[:, 0]
    imag_part = efield[:, 1]
    resid_real = source_term[:, 0] - (curled[:, 0] - coupling * imag_part)
    resid_imag = source_term[:, 1] - (curled[:, 1] + coupling * real_part)
    modulus = 16.0 + coupling * coupling
    update_real = (4.0 * resid_real + coupling * resid_imag) / modulus
    update_imag = (4.0 * resid_imag - coupling * resid_real) / modulus
    return efield + THETA * jnp.stack([update_real, update_imag], axis=1)


def make_source(tx_cells, tx_count, wave_scale, x_start, slab_width, size_y, size_z):
    plane_size = size_y * size_z
    cell_x = tx_cells // plane_size - x_start
    remainder = tx_cells % plane_size
    cell_y = remainder // size_z
    cell_z = remainder % size_z
    active = (jnp.arange(tx_cells.shape[0]) < tx_count[0]) & (cell_x >= 0) & (cell_x < slab_width)
    weights = jnp.where(active, 1.0, 0.0).astype(jnp.float32)
    counts = jnp.zeros((slab_width, size_y, size_z), jnp.float32)
    counts = counts.at[jnp.clip(cell_x, 0, slab_width - 1), cell_y, cell_z].add(weights)
    imag_x = SOURCE_GAIN * wave_scale[:, None, None, None] * counts[None]
    blank = jnp.zeros_like(imag_x)
    real_block = jnp.stack([blank, blank, blank], axis=1)
    imag_block = jnp.stack([imag_x, blank, blank], axis=1)
    return jnp.stack([real_block, imag_block], axis=1)


def adjoint_source(efield, observed):
    differ = efield - observed.astype(jnp.float32)
    return jnp.stack([differ[:, 0], -differ[:, 1]], axis=1)


def gradient_terms(efield, adjoint, wave_scale):
    product = adjoint[:, 0] * efield[:, 1] + adjoint[:, 1] * efield[:, 0]
    weighted = wave_scale[:, None, None, None, None] * product
    horizontal = jnp.sum(weighted[:, 0] + weighted[:, 1], axis=0)
    vertical = jnp.sum(weighted[:, 2], axis=0)
    return jnp.stack([horizontal, vertical])


def inside_mask(first, width, total_x):
    positions = first + jnp.arange(width)
    return ((positions >= 0) & (positions < total_x)).astype(jnp.float32)[:, None, None]


def local_sweep(efield, source_term, sig_pair, wave_scale, inside_pad):
    padded = padded_2(efield, (("gx", 3),), 1)
    curled = curl_masked(padded, inside_pad)[:, :, :, 1:-1]
    return relax(efield, curled, source_term, sig_pair, wave_scale)


def on_device(
    sigma_h, sigma_v, wave_scale, field_start, adjoint_start, observed, tx_count, tx_cells
):
    slab_width = sigma_h.shape[0]
    size_y = sigma_h.shape[1]
    size_z = sigma_h.shape[2]
    slab_index = lax.axis_index("gx")
    total_x = slab_width * lax.axis_size("gx")
    slab_first = slab_index * slab_width
    sig_pair = jnp.stack([sigma_h, sigma_v])
    efield = field_start.astype(jnp.float32)
    adjoint = adjoint_start.astype(jnp.float32)
    inside_pad = inside_mask(slab_first - 1, slab_width + 2, total_x)
    source_term = make_source(
        tx_cells, tx_count, wave_scale, slab_first, slab_width, size_y, size_z
    )
    for sweep in range(ITERS):
        efield = local_sweep(efield, source_term, sig_pair, wave_scale, inside_pad)
    adjoint_rhs = adjoint_source(efield, observed)
    for sweep in range(ITERS):
        adjoint = local_sweep(adjoint, adjoint_rhs, sig_pair, wave_scale, inside_pad)
    local_grad = gradient_terms(efield, adjoint, wave_scale)
    summed = lax.psum(local_grad, "freq")
    share_rows = size_y // lax.axis_size("freq")
    gradient = lax.dynamic_slice_in_dim(summed, lax.axis_index("freq") * share_rows, share_rows, 2)
    return (gradient, efield)


def solution(mesh):
    placed = (
        P("gx", None, None),
        P("gx", None, None),
        P("freq"),
        P("freq", None, None, "gx", None, None),
        P("freq", None, None, "gx", None, None),
        P("freq", None, None, "gx", None, None),
        P(),
        P(),
    )
    return jax.shard_map(
        on_device,
        mesh=mesh,
        in_specs=placed,
        out_specs=(P(None, "gx", "freq", None), P("freq", None, None, "gx", None, None)),
        check_vma=False,
    )
```

profile of v0, /device:TPU:1, one launch (start us, length us, event | category | flops | bytes accessed | tf_op | source)
XLA Modules:
  0.0 269.4 jit_solution(7268834031824373260)
XLA Ops:
  7.2 1.2 fusion.149
  8.4 0.8 copy.50
  9.2 4.7 %collective-permute-start = (f32[1,2,3,1,64,256]{5,4,3,1,2,0:T(8,128)}, f32[1,2,3,1,64,256]{5,4,3,1,2,0:T(8,128)}, u32[]{:S(2)}, u32[]{:S(2)}) collective-permute-start(f32[1,2,3,1,64,256]{5,4,3,1,2,0:T(8,128)} %copy.50), channel_id=1, source_target_pairs={{0,1},{1,2},{2,3},{3,4},{4,5},{5,6},{6,7},{7,8},{8,9},{9,10},{10,1... | collective-permute-start | bytes 1179656 | tf_op jit(solution)/shard_map/ppermute | solution.py:19
  13.9 0.8 copy.51
  14.7 1.4 collective-permute-start.1
  16.3 1.0 fusion.147
  17.3 4.7 %collective-permute-start.4 = (f32[1,2,3,1,64,256]{5,4,3,1,2,0:T(8,128)}, f32[1,2,3,1,64,256]{5,4,3,1,2,0:T(8,128)}, u32[]{:S(2)}, u32[]{:S(2)}) collective-permute-start(f32[1,2,3,1,64,256]{5,4,3,1,2,0:T(8,128)} %get-tuple-element.30), channel_id=1, source_target_pairs={{0,1},{1,2},{2,3},{3,4},{4,5},{5,6},{6,7},{7,8},{8,9},{9,10},{10,1... | collective-permute-start | bytes 1179656 | tf_op jit(solution)/shard_map/ppermute | solution.py:19
  22.0 1.3 collective-permute-start.5
  24.0 1.3 convert_element_type.71
  26.0 4.6 %scatter_fusion = f32[4,64,256]{2,1,0:T(8,128)S(1)} fusion(f32[4,64,256]{2,1,0:T(8,128)S(1)} %broadcast_in_dim.16, s32[64]{0:T(128)S(1)} %fusion.137, f32[64]{0:T(128)S(1)} %get-tuple-element.14), kind=kCustom, calls=%fused_computation | custom fusion | flops 64 | bytes 1536 | tf_op jit(solution)/shard_map/scatter-add | solution.py:79
  30.7 1.0 constant_dynamic-update-slice_fusion.2
  31.9 1.0 constant_dynamic-update-slice_fusion
  33.1 0.6 fusion.6
  33.8 0.6 fusion.9
  34.8 0.6 copy-done.4
  36.3 4.0 %collective-permute-start.2 = (f32[1,2,3,1,64,256]{5,4,3,1,2,0:T(8,128)S(1)}, f32[1,2,3,1,64,256]{5,4,3,1,2,0:T(8,128)S(1)}, u32[]{:S(2)}, u32[]{:S(2)}) collective-permute-start(f32[1,2,3,1,64,256]{5,4,3,1,2,0:T(8,128)S(1)} %copy.52), channel_id=1, source_target_pairs={{0,1},{1,2},{2,3},{3,4},{4,5},{5,6},{6,7},{7,8},{8,9},{9,10},{10,1... | collective-permute-start | bytes 1179656 | tf_op jit(solution)/shard_map/ppermute | solution.py:19
  40.3 1.3 collective-permute-start.3
  41.6 3.1 %collective-permute-done.4 = f32[1,2,3,1,64,256]{5,4,3,1,2,0:T(8,128)} collective-permute-done((f32[1,2,3,1,64,256]{5,4,3,1,2,0:T(8,128)}, f32[1,2,3,1,64,256]{5,4,3,1,2,0:T(8,128)}, u32[]{:S(2)}, u32[]{:S(2)}) %collective-permute-start.4) | collective-permute-done | bytes 393248 | tf_op jit(solution)/shard_map/ppermute | solution.py:19
  44.7 1.4 pad_maximum_fusion
  46.4 5.5 %collective-permute-done.2 = f32[1,2,3,1,64,256]{5,4,3,1,2,0:T(8,128)S(1)} collective-permute-done((f32[1,2,3,1,64,256]{5,4,3,1,2,0:T(8,128)S(1)}, f32[1,2,3,1,64,256]{5,4,3,1,2,0:T(8,128)S(1)}, u32[]{:S(2)}, u32[]{:S(2)}) %collective-permute-start.2) | collective-permute-done | bytes 393248 | tf_op jit(solution)/shard_map/ppermute | solution.py:19
  52.2 5.0 %collective-permute-done.3 = f32[1,2,3,1,64,256]{5,4,3,1,2,0:T(8,128)S(1)} collective-permute-done((f32[1,2,3,1,64,256]{5,4,3,1,2,0:T(8,128)S(1)}, f32[1,2,3,1,64,256]{5,4,3,1,2,0:T(8,128)S(1)}, u32[]{:S(2)}, u32[]{:S(2)}) %collective-permute-start.3) | collective-permute-done | bytes 393248 | tf_op jit(solution)/shard_map/ppermute | solution.py:21
  57.4 1.4 fusion.30
  58.9 0.5 fusion.33
  60.6 0.9 copy-done.6
  62.9 5.8 %collective-permute-start.6 = (f32[1,2,3,1,64,256]{5,4,3,1,2,0:T(8,128)S(1)}, f32[1,2,3,1,64,256]{5,4,3,1,2,0:T(8,128)S(1)}, u32[]{:S(2)}, u32[]{:S(2)}) collective-permute-start(f32[1,2,3,1,64,256]{5,4,3,1,2,0:T(8,128)S(1)} %get-tuple-element.29), channel_id=1, source_target_pairs={{0,1},{1,2},{2,3},{3,4},{4,5},{5,6},{6,7},{7,8},{8,9},{9,10},{10,1... | collective-permute-start | bytes 1179656 | tf_op jit(solution)/shard_map/ppermute | solution.py:19
  69.1 1.5 collective-permute-start.7
  70.8 2.6 collective-permute-done.6
  73.7 15.4 %collective-permute-done.7 = f32[1,2,3,1,64,256]{5,4,3,1,2,0:T(8,128)S(1)} collective-permute-done((f32[1,2,3,1,64,256]{5,4,3,1,2,0:T(8,128)S(1)}, f32[1,2,3,1,64,256]{5,4,3,1,2,0:T(8,128)S(1)}, u32[]{:S(2)}, u32[]{:S(2)}) %collective-permute-start.7) | collective-permute-done | bytes 393248 | tf_op jit(solution)/shard_map/ppermute | solution.py:21
  89.4 0.6 fusion.42
  92.1 0.8 pad_maximum_fusion.9
  92.9 168.2 %all-reduce.51.cloned.1.call-done = f32[2,4,64,256]{3,2,1,0:T(8,128)} async-done(((f32[2,4,64,256]{3,2,1,0:T(8,128)}), f32[2,4,64,256]{3,2,1,0:T(8,128)}) %all-reduce.51.cloned.1.call-update) | async-done | bytes 524304 | tf_op jit(solution)/shard_map/psum | solution.py:133
  261.1 1.5 constant_dynamic-slice_fusion
  (57 shorter events, 8.4 us)
Async XLA Ops:
  7.2 8.9 %copy-start.3 = (bf16[1,2,3,4,64,256]{5,4,3,2,1,0:T(8,128)(2,1)S(1)}, bf16[1,2,3,4,64,256]{5,4,3,2,1,0:T(8,128)(2,1)}, u32[]{:S(2)}) copy-start(bf16[1,2,3,4,64,256]{5,4,3,2,1,0:T(8,128)(2,1)} %param.12) | copy-start | bytes 2359300
  7.2 253.9 %all-reduce.51.cloned.1.call-start = ((), (), s32[]{:S(2)}) async-start(), calls=%async_computation | async-start | bytes 1048576 | tf_op jit(solution)/shard_map/psum | solution.py:133
  9.2 21.5 %collective-permute-start = (f32[1,2,3,1,64,256]{5,4,3,1,2,0:T(8,128)}, f32[1,2,3,1,64,256]{5,4,3,1,2,0:T(8,128)}, u32[]{:S(2)}, u32[]{:S(2)}) collective-permute-start(f32[1,2,3,1,64,256]{5,4,3,1,2,0:T(8,128)} %copy.50), channel_id=1, source_target_pairs={{0,1},{1,2},{2,3},{3,4},{4,5},{5,6},{6,7},{7,8},{8,9},{9,10},{10,1... | collective-permute-start | bytes 1179656 | tf_op jit(solution)/shard_map/ppermute | solution.py:19
  14.7 9.3 %copy-start.7 = (s32[64]{0:T(128)S(1)}, s32[64]{0:T(128)}, u32[]{:S(2)}) copy-start(s32[64]{0:T(128)} %param.15) | copy-start | bytes 772
  14.7 9.3 %copy-start = (bf16[1,2,3,4,64,256]{5,4,3,2,1,0:T(8,128)(2,1)S(1)}, bf16[1,2,3,4,64,256]{5,4,3,2,1,0:T(8,128)(2,1)}, u32[]{:S(2)}) copy-start(bf16[1,2,3,4,64,256]{5,4,3,2,1,0:T(8,128)(2,1)} %param.11) | copy-start | bytes 2359300
  14.7 17.2 %collective-permute-start.1 = (f32[1,2,3,1,64,256]{5,4,3,1,2,0:T(8,128)}, f32[1,2,3,1,64,256]{5,4,3,1,2,0:T(8,128)}, u32[]{:S(2)}, u32[]{:S(2)}) collective-permute-start(f32[1,2,3,1,64,256]{5,4,3,1,2,0:T(8,128)} %copy.51), channel_id=1, source_target_pairs={{1,0},{2,1},{3,2},{4,3},{5,4},{6,5},{7,6},{8,7},{9,8},{10,9},{11,1... | collective-permute-start | bytes 1179656 | tf_op jit(solution)/shard_map/ppermute | solution.py:21
  17.3 27.4 %collective-permute-start.4 = (f32[1,2,3,1,64,256]{5,4,3,1,2,0:T(8,128)}, f32[1,2,3,1,64,256]{5,4,3,1,2,0:T(8,128)}, u32[]{:S(2)}, u32[]{:S(2)}) collective-permute-start(f32[1,2,3,1,64,256]{5,4,3,1,2,0:T(8,128)} %get-tuple-element.30), channel_id=1, source_target_pairs={{0,1},{1,2},{2,3},{3,4},{4,5},{5,6},{6,7},{7,8},{8,9},{9,10},{10,1... | collective-permute-start | bytes 1179656 | tf_op jit(solution)/shard_map/ppermute | solution.py:19
  22.0 22.7 %collective-permute-start.5 = (f32[1,2,3,1,64,256]{5,4,3,1,2,0:T(8,128)}, f32[1,2,3,1,64,256]{5,4,3,1,2,0:T(8,128)}, u32[]{:S(2)}, u32[]{:S(2)}) collective-permute-start(f32[1,2,3,1,64,256]{5,4,3,1,2,0:T(8,128)} %get-tuple-element.31), channel_id=1, source_target_pairs={{1,0},{2,1},{3,2},{4,3},{5,4},{6,5},{7,6},{8,7},{9,8},{10,9},{11,1... | collective-permute-start | bytes 1179656 | tf_op jit(solution)/shard_map/ppermute | solution.py:21
  33.7 1.0 copy-start.1
  33.7 1.0 copy-start.2
  33.8 1.6 copy-start.4
  36.3 15.6 %collective-permute-start.2 = (f32[1,2,3,1,64,256]{5,4,3,1,2,0:T(8,128)S(1)}, f32[1,2,3,1,64,256]{5,4,3,1,2,0:T(8,128)S(1)}, u32[]{:S(2)}, u32[]{:S(2)}) collective-permute-start(f32[1,2,3,1,64,256]{5,4,3,1,2,0:T(8,128)S(1)} %copy.52), channel_id=1, source_target_pairs={{0,1},{1,2},{2,3},{3,4},{4,5},{5,6},{6,7},{7,8},{8,9},{9,10},{10,1... | collective-permute-start | bytes 1179656 | tf_op jit(solution)/shard_map/ppermute | solution.py:19
  40.3 16.9 %collective-permute-start.3 = (f32[1,2,3,1,64,256]{5,4,3,1,2,0:T(8,128)S(1)}, f32[1,2,3,1,64,256]{5,4,3,1,2,0:T(8,128)S(1)}, u32[]{:S(2)}, u32[]{:S(2)}) collective-permute-start(f32[1,2,3,1,64,256]{5,4,3,1,2,0:T(8,128)S(1)} %copy.53), channel_id=1, source_target_pairs={{1,0},{2,1},{3,2},{4,3},{5,4},{6,5},{7,6},{8,7},{9,8},{10,9},{11,1... | collective-permute-start | bytes 1179656 | tf_op jit(solution)/shard_map/ppermute | solution.py:21
  60.4 1.1 copy-start.6
  62.9 10.5 %collective-permute-start.6 = (f32[1,2,3,1,64,256]{5,4,3,1,2,0:T(8,128)S(1)}, f32[1,2,3,1,64,256]{5,4,3,1,2,0:T(8,128)S(1)}, u32[]{:S(2)}, u32[]{:S(2)}) collective-permute-start(f32[1,2,3,1,64,256]{5,4,3,1,2,0:T(8,128)S(1)} %get-tuple-element.29), channel_id=1, source_target_pairs={{0,1},{1,2},{2,3},{3,4},{4,5},{5,6},{6,7},{7,8},{8,9},{9,10},{10,1... | collective-permute-start | bytes 1179656 | tf_op jit(solution)/shard_map/ppermute | solution.py:19
  69.1 22.6 %copy-start.5 = (f32[1,2,3,4,64,256]{5,4,3,2,1,0:T(8,128)}, f32[1,2,3,4,64,256]{5,4,3,2,1,0:T(8,128)S(1)}, u32[]{:S(2)}) copy-start(f32[1,2,3,4,64,256]{5,4,3,2,1,0:T(8,128)S(1)} %fusion.1) | copy-start | bytes 4718596
  69.1 20.0 %collective-permute-start.7 = (f32[1,2,3,1,64,256]{5,4,3,1,2,0:T(8,128)S(1)}, f32[1,2,3,1,64,256]{5,4,3,1,2,0:T(8,128)S(1)}, u32[]{:S(2)}, u32[]{:S(2)}) collective-permute-start(f32[1,2,3,1,64,256]{5,4,3,1,2,0:T(8,128)S(1)} %get-tuple-element.28), channel_id=1, source_target_pairs={{1,0},{2,1},{3,2},{4,3},{5,4},{6,5},{7,6},{8,7},{9,8},{10,9},{11,1... | collective-permute-start | bytes 1179656 | tf_op jit(solution)/shard_map/ppermute | solution.py:21
Sparse Core Ops, SparseCore 0:
  93.0 168.0 all-reduce.50
where the time goes:
time: 270 us; the launch traced here: 269 us
  waiting for transfers between devices  200 us (74%)
  starting transfers between devices  24.8 us (9%)
  other arithmetic  18.7 us (7%)
  between operations  15.8 us (6%)
  local copies, waits for them, and re-layouts  10.3 us (4%)
    psum x1, waiting for transfers between devices, on_device(): summed = lax.psum(local_grad, 'freq')  168 us
    ppermute x4, waiting for transfers between devices, padded_2(): lax.ppermute(head, axis, [((i + 1) % count, i) for i in range(ends)])  20.4 us
    ppermute x4, starting transfers between devices, padded_2(): lax.ppermute(tail, axis, [(i, (i + 1) % count) for i in range(ends)])  19.3 us
    ppermute x4, waiting for transfers between devices, padded_2(): lax.ppermute(tail, axis, [(i, (i + 1) % count) for i in range(ends)])  11.2 us
    ppermute x4, starting transfers between devices, padded_2(): lax.ppermute(head, axis, [((i + 1) % count, i) for i in range(ends)])  5.46 us
  transfers between devices with their start and end apart: 9, of which 6 were waited for; matrix products, arithmetic and copies ran while one was open for 6% of the time, Pallas kernels for 0%

commit v1 on v0

--- a/solution.py
+++ b/solution.py
@@ -130,7 +130,7 @@
     for sweep in range(ITERS):
         adjoint = local_sweep(adjoint, adjoint_rhs, sig_pair, wave_scale, inside_pad)
     local_grad = gradient_terms(efield, adjoint, wave_scale)
-    summed = lax.psum(local_grad, "freq")
+    summed = lax.all_gather(local_grad, "freq").sum(axis=0)
     share_rows = size_y // lax.axis_size("freq")
     gradient = lax.dynamic_slice_in_dim(summed, lax.axis_index("freq") * share_rows, share_rows, 2)
     return (gradient, efield)

time: 270 us -> 208 us (0.77)
  waiting for transfers between devices: 200 us -> 134 us
  other arithmetic: 18.7 us -> 23.4 us
    psum x1 -> x0, waiting for transfers between devices: 168 us -> none  [on_device(): summed = lax.psum(local_grad, 'freq')]
    all_gather x0 -> x1, waiting for transfers between devices: none -> 103 us  [on_device(): summed = lax.all_gather(local_grad, 'freq').sum(axis=0)]
    reduce_sum x0 -> x1, other arithmetic: none -> 4.01 us  [on_device(): summed = lax.all_gather(local_grad, 'freq').sum(axis=0)]
  transfers between devices with their start and end apart: 9 -> 9, of which waited for: 6 -> 6; matrix products, arithmetic and copies ran while one was open for 6% -> 7% of each run, Pallas kernels for 0% -> 0%
where the time goes in v1:
time: 208 us
  waiting for transfers between devices  134 us (64%)
  starting transfers between devices  24.8 us (12%)
  other arithmetic  23.4 us (11%)
  between operations  15.8 us (8%)
  local copies, waits for them, and re-layouts  9.33 us (4%)
    all_gather x1, waiting for transfers between devices, on_device(): summed = lax.all_gather(local_grad, 'freq').sum(axis=0)  103 us
    ppermute x4, waiting for transfers between devices, padded_2(): lax.ppermute(head, axis, [((i + 1) % count, i) for i in range(ends)])  20.5 us
    ppermute x4, starting transfers between devices, padded_2(): lax.ppermute(tail, axis, [(i, (i + 1) % count) for i in range(ends)])  19.3 us
    ppermute x4, waiting for transfers between devices, padded_2(): lax.ppermute(tail, axis, [(i, (i + 1) % count) for i in range(ends)])  11 us
    ppermute x4, starting transfers between devices, padded_2(): lax.ppermute(head, axis, [((i + 1) % count, i) for i in range(ends)])  5.46 us
    unnamed x23, local copies, waits for them, and re-layouts  4.64 us
    scatter-add x1, other arithmetic, make_source(): counts.at[jnp.clip(cell_x, 0, slab_width - 1), cell_y, cell_z].add(weights)  4.6 us
  transfers between devices with their start and end apart: 9, of which 6 were waited for; matrix products, arithmetic and copies ran while one was open for 7% of the time, Pallas kernels for 0%

profile of v1, /device:TPU:1, one launch (start us, length us, event | category | flops | bytes accessed | tf_op | source)
XLA Modules:
  0.0 207.7 jit_solution(2720383016536498574)
XLA Ops:
  7.2 1.2 fusion.149
  8.4 0.8 copy.83
  9.2 4.7 %collective-permute-start = (f32[1,2,3,1,64,256]{5,4,3,1,2,0:T(8,128)}, f32[1,2,3,1,64,256]{5,4,3,1,2,0:T(8,128)}, u32[]{:S(2)}, u32[]{:S(2)}) collective-permute-start(f32[1,2,3,1,64,256]{5,4,3,1,2,0:T(8,128)} %copy.83), channel_id=1, source_target_pairs={{0,1},{1,2},{2,3},{3,4},{4,5},{5,6},{6,7},{7,8},{8,9},{9,10},{10,1... | collective-permute-start | bytes 1179656 | tf_op jit(solution)/shard_map/ppermute | solution.py:19
  13.9 0.8 copy.84
  14.7 1.4 collective-permute-start.1
  16.3 1.0 fusion.147
  17.3 4.7 %collective-permute-start.4 = (f32[1,2,3,1,64,256]{5,4,3,1,2,0:T(8,128)}, f32[1,2,3,1,64,256]{5,4,3,1,2,0:T(8,128)}, u32[]{:S(2)}, u32[]{:S(2)}) collective-permute-start(f32[1,2,3,1,64,256]{5,4,3,1,2,0:T(8,128)} %get-tuple-element.30), channel_id=1, source_target_pairs={{0,1},{1,2},{2,3},{3,4},{4,5},{5,6},{6,7},{7,8},{8,9},{9,10},{10,1... | collective-permute-start | bytes 1179656 | tf_op jit(solution)/shard_map/ppermute | solution.py:19
  22.0 1.3 collective-permute-start.5
  24.0 1.3 convert_element_type.71
  26.0 4.6 %scatter_fusion = f32[4,64,256]{2,1,0:T(8,128)S(1)} fusion(f32[4,64,256]{2,1,0:T(8,128)S(1)} %broadcast_in_dim.16, s32[64]{0:T(128)S(1)} %fusion.137, f32[64]{0:T(128)S(1)} %get-tuple-element.14), kind=kCustom, calls=%fused_computation | custom fusion | flops 64 | bytes 1536 | tf_op jit(solution)/shard_map/scatter-add | solution.py:79
  30.7 1.0 constant_dynamic-update-slice_fusion.2
  31.9 1.0 constant_dynamic-update-slice_fusion
  33.1 0.6 fusion.6
  36.3 4.0 %collective-permute-start.2 = (f32[1,2,3,1,64,256]{5,4,3,1,2,0:T(8,128)S(1)}, f32[1,2,3,1,64,256]{5,4,3,1,2,0:T(8,128)S(1)}, u32[]{:S(2)}, u32[]{:S(2)}) collective-permute-start(f32[1,2,3,1,64,256]{5,4,3,1,2,0:T(8,128)S(1)} %copy.85), channel_id=1, source_target_pairs={{0,1},{1,2},{2,3},{3,4},{4,5},{5,6},{6,7},{7,8},{8,9},{9,10},{10,1... | collective-permute-start | bytes 1179656 | tf_op jit(solution)/shard_map/ppermute | solution.py:19
  40.4 1.3 collective-permute-start.3
  41.6 3.0 %collective-permute-done.4 = f32[1,2,3,1,64,256]{5,4,3,1,2,0:T(8,128)} collective-permute-done((f32[1,2,3,1,64,256]{5,4,3,1,2,0:T(8,128)}, f32[1,2,3,1,64,256]{5,4,3,1,2,0:T(8,128)}, u32[]{:S(2)}, u32[]{:S(2)}) %collective-permute-start.4) | collective-permute-done | bytes 393248 | tf_op jit(solution)/shard_map/ppermute | solution.py:19
  44.7 1.4 pad_maximum_fusion
  46.4 5.5 %collective-permute-done.2 = f32[1,2,3,1,64,256]{5,4,3,1,2,0:T(8,128)S(1)} collective-permute-done((f32[1,2,3,1,64,256]{5,4,3,1,2,0:T(8,128)S(1)}, f32[1,2,3,1,64,256]{5,4,3,1,2,0:T(8,128)S(1)}, u32[]{:S(2)}, u32[]{:S(2)}) %collective-permute-start.2) | collective-permute-done | bytes 393248 | tf_op jit(solution)/shard_map/ppermute | solution.py:19
  52.2 5.0 %collective-permute-done.3 = f32[1,2,3,1,64,256]{5,4,3,1,2,0:T(8,128)S(1)} collective-permute-done((f32[1,2,3,1,64,256]{5,4,3,1,2,0:T(8,128)S(1)}, f32[1,2,3,1,64,256]{5,4,3,1,2,0:T(8,128)S(1)}, u32[]{:S(2)}, u32[]{:S(2)}) %collective-permute-start.3) | collective-permute-done | bytes 393248 | tf_op jit(solution)/shard_map/ppermute | solution.py:21
  57.4 1.5 fusion.30
  60.8 0.9 copy-done.6
  61.7 0.6 copy_subtract_fusion
  63.1 5.8 %collective-permute-start.6 = (f32[1,2,3,1,64,256]{5,4,3,1,2,0:T(8,128)S(1)}, f32[1,2,3,1,64,256]{5,4,3,1,2,0:T(8,128)S(1)}, u32[]{:S(2)}, u32[]{:S(2)}) collective-permute-start(f32[1,2,3,1,64,256]{5,4,3,1,2,0:T(8,128)S(1)} %get-tuple-element.29), channel_id=1, source_target_pairs={{0,1},{1,2},{2,3},{3,4},{4,5},{5,6},{6,7},{7,8},{8,9},{9,10},{10,1... | collective-permute-start | bytes 1179656 | tf_op jit(solution)/shard_map/ppermute | solution.py:19
  69.4 1.5 collective-permute-start.7
  71.1 2.5 %collective-permute-done.6 = f32[1,2,3,1,64,256]{5,4,3,1,2,0:T(8,128)S(1)} collective-permute-done((f32[1,2,3,1,64,256]{5,4,3,1,2,0:T(8,128)S(1)}, f32[1,2,3,1,64,256]{5,4,3,1,2,0:T(8,128)S(1)}, u32[]{:S(2)}, u32[]{:S(2)}) %collective-permute-start.6) | collective-permute-done | bytes 393248 | tf_op jit(solution)/shard_map/ppermute | solution.py:19
  73.9 15.5 %collective-permute-done.7 = f32[1,2,3,1,64,256]{5,4,3,1,2,0:T(8,128)S(1)} collective-permute-done((f32[1,2,3,1,64,256]{5,4,3,1,2,0:T(8,128)S(1)}, f32[1,2,3,1,64,256]{5,4,3,1,2,0:T(8,128)S(1)}, u32[]{:S(2)}, u32[]{:S(2)}) %collective-permute-start.7) | collective-permute-done | bytes 393248 | tf_op jit(solution)/shard_map/ppermute | solution.py:21
  89.6 0.7 fusion.42
  90.8 0.6 add_divide_fusion
  92.4 0.9 pad_maximum_fusion.9
  93.4 102.9 %all-gather.3.cloned.1.call-done = f32[32,4,64,256]{3,2,1,0:T(8,128)} async-done(((f32[2,4,64,256]{3,2,1,0:T(8,128)}), f32[32,4,64,256]{3,2,1,0:T(8,128)}) %all-gather.3.cloned.1.call-update) | async-done | bytes 8388624 | tf_op jit(solution)/shard_map/all_gather | solution.py:133
  196.2 4.0 %reduce_sum.8 = f32[2,4,64,256]{3,2,1,0:T(8,128)S(1)} reduce(f32[16,2,4,64,256]{4,3,2,1,0:T(8,128)} %bitcast.231, f32[]{:T(128)} %constant.71.clone.1), dimensions={0}, to_apply=%region_1.2 | reduce | flops 1966080 | bytes 8912900 | tf_op jit(solution)/shard_map/reduce_sum | solution.py:133
  200.2 0.6 constant_dynamic-slice_fusion
  (58 shorter events, 9.3 us)
Async XLA Ops:
  7.2 8.9 %copy-start.3 = (bf16[1,2,3,4,64,256]{5,4,3,2,1,0:T(8,128)(2,1)S(1)}, bf16[1,2,3,4,64,256]{5,4,3,2,1,0:T(8,128)(2,1)}, u32[]{:S(2)}) copy-start(bf16[1,2,3,4,64,256]{5,4,3,2,1,0:T(8,128)(2,1)} %param.12) | copy-start | bytes 2359300
  7.2 189.1 %all-gather.3.cloned.1.call-start = ((), (), s32[]{:S(2)}) async-start(), calls=%async_computation | async-start | bytes 8912896 | tf_op jit(solution)/shard_map/all_gather | solution.py:133
  9.2 21.5 %collective-permute-start = (f32[1,2,3,1,64,256]{5,4,3,1,2,0:T(8,128)}, f32[1,2,3,1,64,256]{5,4,3,1,2,0:T(8,128)}, u32[]{:S(2)}, u32[]{:S(2)}) collective-permute-start(f32[1,2,3,1,64,256]{5,4,3,1,2,0:T(8,128)} %copy.83), channel_id=1, source_target_pairs={{0,1},{1,2},{2,3},{3,4},{4,5},{5,6},{6,7},{7,8},{8,9},{9,10},{10,1... | collective-permute-start | bytes 1179656 | tf_op jit(solution)/shard_map/ppermute | solution.py:19
  14.7 9.3 %copy-start.7 = (s32[64]{0:T(128)S(1)}, s32[64]{0:T(128)}, u32[]{:S(2)}) copy-start(s32[64]{0:T(128)} %param.15) | copy-start | bytes 772
  14.7 9.3 %copy-start = (bf16[1,2,3,4,64,256]{5,4,3,2,1,0:T(8,128)(2,1)S(1)}, bf16[1,2,3,4,64,256]{5,4,3,2,1,0:T(8,128)(2,1)}, u32[]{:S(2)}) copy-start(bf16[1,2,3,4,64,256]{5,4,3,2,1,0:T(8,128)(2,1)} %param.11) | copy-start | bytes 2359300
  14.7 17.2 %collective-permute-start.1 = (f32[1,2,3,1,64,256]{5,4,3,1,2,0:T(8,128)}, f32[1,2,3,1,64,256]{5,4,3,1,2,0:T(8,128)}, u32[]{:S(2)}, u32[]{:S(2)}) collective-permute-start(f32[1,2,3,1,64,256]{5,4,3,1,2,0:T(8,128)} %copy.84), channel_id=1, source_target_pairs={{1,0},{2,1},{3,2},{4,3},{5,4},{6,5},{7,6},{8,7},{9,8},{10,9},{11,1... | collective-permute-start | bytes 1179656 | tf_op jit(solution)/shard_map/ppermute | solution.py:21
  17.3 27.4 %collective-permute-start.4 = (f32[1,2,3,1,64,256]{5,4,3,1,2,0:T(8,128)}, f32[1,2,3,1,64,256]{5,4,3,1,2,0:T(8,128)}, u32[]{:S(2)}, u32[]{:S(2)}) collective-permute-start(f32[1,2,3,1,64,256]{5,4,3,1,2,0:T(8,128)} %get-tuple-element.30), channel_id=1, source_target_pairs={{0,1},{1,2},{2,3},{3,4},{4,5},{5,6},{6,7},{7,8},{8,9},{9,10},{10,1... | collective-permute-start | bytes 1179656 | tf_op jit(solution)/shard_map/ppermute | solution.py:19
  22.0 22.7 %collective-permute-start.5 = (f32[1,2,3,1,64,256]{5,4,3,1,2,0:T(8,128)}, f32[1,2,3,1,64,256]{5,4,3,1,2,0:T(8,128)}, u32[]{:S(2)}, u32[]{:S(2)}) collective-permute-start(f32[1,2,3,1,64,256]{5,4,3,1,2,0:T(8,128)} %get-tuple-element.31), channel_id=1, source_target_pairs={{1,0},{2,1},{3,2},{4,3},{5,4},{6,5},{7,6},{8,7},{9,8},{10,9},{11,1... | collective-permute-start | bytes 1179656 | tf_op jit(solution)/shard_map/ppermute | solution.py:21
  33.7 1.0 copy-start.1
  33.7 1.0 copy-start.2
  33.8 1.6 copy-start.4
  36.3 15.6 %collective-permute-start.2 = (f32[1,2,3,1,64,256]{5,4,3,1,2,0:T(8,128)S(1)}, f32[1,2,3,1,64,256]{5,4,3,1,2,0:T(8,128)S(1)}, u32[]{:S(2)}, u32[]{:S(2)}) collective-permute-start(f32[1,2,3,1,64,256]{5,4,3,1,2,0:T(8,128)S(1)} %copy.85), channel_id=1, source_target_pairs={{0,1},{1,2},{2,3},{3,4},{4,5},{5,6},{6,7},{7,8},{8,9},{9,10},{10,1... | collective-permute-start | bytes 1179656 | tf_op jit(solution)/shard_map/ppermute | solution.py:19
  40.4 16.9 %collective-permute-start.3 = (f32[1,2,3,1,64,256]{5,4,3,1,2,0:T(8,128)S(1)}, f32[1,2,3,1,64,256]{5,4,3,1,2,0:T(8,128)S(1)}, u32[]{:S(2)}, u32[]{:S(2)}) collective-permute-start(f32[1,2,3,1,64,256]{5,4,3,1,2,0:T(8,128)S(1)} %copy.86), channel_id=1, source_target_pairs={{1,0},{2,1},{3,2},{4,3},{5,4},{6,5},{7,6},{8,7},{9,8},{10,9},{11,1... | collective-permute-start | bytes 1179656 | tf_op jit(solution)/shard_map/ppermute | solution.py:21
  60.5 1.1 copy-start.6
  63.1 10.5 %collective-permute-start.6 = (f32[1,2,3,1,64,256]{5,4,3,1,2,0:T(8,128)S(1)}, f32[1,2,3,1,64,256]{5,4,3,1,2,0:T(8,128)S(1)}, u32[]{:S(2)}, u32[]{:S(2)}) collective-permute-start(f32[1,2,3,1,64,256]{5,4,3,1,2,0:T(8,128)S(1)} %get-tuple-element.29), channel_id=1, source_target_pairs={{0,1},{1,2},{2,3},{3,4},{4,5},{5,6},{6,7},{7,8},{8,9},{9,10},{10,1... | collective-permute-start | bytes 1179656 | tf_op jit(solution)/shard_map/ppermute | solution.py:19
  69.4 22.7 %copy-start.5 = (f32[1,2,3,4,64,256]{5,4,3,2,1,0:T(8,128)}, f32[1,2,3,4,64,256]{5,4,3,2,1,0:T(8,128)S(1)}, u32[]{:S(2)}) copy-start(f32[1,2,3,4,64,256]{5,4,3,2,1,0:T(8,128)S(1)} %fusion.1) | copy-start | bytes 4718596
  69.4 20.0 %collective-permute-start.7 = (f32[1,2,3,1,64,256]{5,4,3,1,2,0:T(8,128)S(1)}, f32[1,2,3,1,64,256]{5,4,3,1,2,0:T(8,128)S(1)}, u32[]{:S(2)}, u32[]{:S(2)}) collective-permute-start(f32[1,2,3,1,64,256]{5,4,3,1,2,0:T(8,128)S(1)} %get-tuple-element.28), channel_id=1, source_target_pairs={{1,0},{2,1},{3,2},{4,3},{5,4},{6,5},{7,6},{8,7},{9,8},{10,9},{11,1... | collective-permute-start | bytes 1179656 | tf_op jit(solution)/shard_map/ppermute | solution.py:21
Sparse Core Ops, SparseCore 0:
  93.5 102.6 all-gather.2
